TPU v7x, 32 devices: a whole 2x2x4 slice. The times are simulated.
32 devices in a mesh: dp: 8 (over y, x, core), mp: 4 (over z).
Axes of the slice: x: 2, y: 2, z: 4, core: 2. Of those that a mesh axis runs over, the one named last changes fastest.
Arguments:
- tokens: bfloat16 [2, 1024, 4096], P(None, 'dp', 'mp'), may hold values from -6 to 6
- targets: bfloat16 [2, 1024, 4096], P(None, 'dp', 'mp'), may hold values from -6 to 6
- weight: bfloat16 [4096, 4096], P('mp'), may hold values from -0.09375 to 0.09375
- basis: bfloat16 [4096, 512], replicated, may hold values from -0.09375 to 0.09375
- moment1: float32 [4, 1024, 512], P('mp', 'dp'), may hold values from -0.06 to 0.06
- moment2: float32 [4, 1024, 512], P('mp', 'dp'), may hold values from 1e-05 to 0.001
Outputs:
- new_weight: bfloat16 [4096, 4096], P('mp')
- new_moment1: float32 [4, 1024, 512], P('mp', 'dp')
- new_moment2: float32 [4, 1024, 512], P('mp', 'dp')
All inputs are finite; a program needn't handle non-finite values.
Results may differ from a plain program's by a relative error of at most 0.009.
Values may be sent and summed in bfloat16 or wider, within the bound.
A program may use at most 64 MiB of HBM per device.

v0:
```python
import jax
import jax.numpy as jnp
from jax import lax
from jax.sharding import PartitionSpec as P


def local(tokens, targets, weight, basis, moment1, moment2):
    whole = lax.all_gather(tokens, "mp", axis=2, tiled=True)
    total_tokens = tokens.shape[1] * lax.axis_size("dp")
    owned_rows = moment1.shape[1]
    first = moment1[0]
    second = moment2[0]
    current = weight
    for turn in range(2):
        inputs = whole[turn]
        outputs = lax.dot_general(
            inputs, current, (((1,), (1,)), ((), ())), preferred_element_type=jnp.float32
        ).astype(jnp.bfloat16)
        errors = (outputs.astype(jnp.float32) - targets[turn].astype(jnp.float32)).astype(
            jnp.bfloat16
        )
        reduced = jnp.dot(inputs, basis, preferred_element_type=jnp.float32)
        part_errors = errors.astype(jnp.float32)
        projected = (
            lax.psum_scatter(
                lax.dot_general(
                    part_errors, reduced, (((0,), (0,)), ((), ())), precision=lax.Precision.HIGHEST
                ),
                "dp",
                scatter_dimension=0,
                tiled=True,
            )
            / total_tokens
        )
        first = 0.9 * first + 0.1 * projected
        second = 0.95 * second + 0.05 * projected * projected
        direction = (first / (jnp.sqrt(second) + 1e-08)).astype(jnp.bfloat16)
        own_weight = lax.dynamic_slice_in_dim(
            current, lax.axis_index("dp") * owned_rows, owned_rows, 0
        )
        lifted = lax.dot_general(
            direction, basis, (((1,), (1,)), ((), ())), preferred_element_type=jnp.float32
        )
        new_rows = (own_weight.astype(jnp.float32) - 0.02 * lifted).astype(jnp.bfloat16)
        current = lax.all_gather(new_rows, "dp", axis=0, tiled=True)
    return (current, first[None], second[None])


def solution(mesh):
    in_specs = (
        P(None, "dp", "mp"),
        P(None, "dp", "mp"),
        P("mp", None),
        P(),
        P("mp", "dp", None),
        P("mp", "dp", None),
    )
    out_specs = (P("mp", None), P("mp", "dp", None), P("mp", "dp", None))
    return jax.shard_map(local, mesh=mesh, in_specs=in_specs, out_specs=out_specs, check_vma=False)
```

profile of v0, /device:TPU:0, one launch (start us, length us, event | category | flops | bytes accessed | tf_op | source)
XLA Modules:
  0.0 293.4 jit_solution(11323379693087445901)
XLA Ops:
  7.2 0.0 copy-start.5
  7.2 0.0 all-gather.4.cloned.1.call-start
  7.2 0.7 all-gather.4.cloned.1.call-update
  7.9 0.0 reduce-scatter.3.cloned.1.call-start
  8.0 50.0 %all-gather.4.cloned.1.call-done = bf16[2,128,4096]{2,1,0:T(8,128)(2,1)} async-done(((bf16[2,128,1024]{2,1,0:T(8,128)(2,1)}), bf16[2,128,4096]{2,1,0:T(8,128)(2,1)}) %all-gather.4.cloned.1.call-update) | async-done | bytes 2097168 | tf_op jit(solution)/shard_map/all_gather | solution.py:8
  58.0 0.0 copy-start
  58.0 3.4 %fusion.11 = f32[128,512]{1,0:T(8,128)S(1)} fusion(bf16[4096,512]{1,0:T(8,128)(2,1)} %param.9, bf16[2,128,4096]{2,1,0:T(8,128)(2,1)} %all-gather.4.cloned.1.call-done), kind=kOutput, calls=%fused_computation.17 | convolution fusion | flops 536870912 | bytes 5505024 | tf_op jit(solution)/shard_map/dot_general | solution.py:22
  61.3 0.0 copy-done.5
  61.4 0.0 copy-done
  61.4 6.3 %fusion.10 = bf16[128,1024]{1,0:T(8,128)(2,1)S(1)} fusion(bf16[1024,4096]{1,0:T(8,128)(2,1)} %param.8, bf16[2,128,4096]{2,1,0:T(8,128)(2,1)S(1)} %copy-done, bf16[2,128,1024]{2,1,0:T(8,128)(2,1)S(1)} %copy-done.5), kind=kOutput, calls=%fused_computation.14 | convolution fusion | flops 1074397184 | bytes 9961472 | tf_op jit(solution)/shard_map/dot_general | solution.py:16
  67.6 0.0 copy-start.1
  67.6 0.0 copy-start.2
  67.7 2.4 fusion.24
  70.0 0.0 reduce-scatter.3.cloned.1.call-update
  70.0 0.0 all-gather.6.cloned.1.call-start
  70.1 40.0 %reduce-scatter.3.cloned.1.call-done = f32[128,512]{1,0:T(8,128)} async-done(((f32[1024,512]{1,0:T(8,128)}), f32[128,512]{1,0:T(8,128)}) %reduce-scatter.3.cloned.1.call-update) | async-done | bytes 262160 | tf_op jit(solution)/shard_map/reduce_scatter | solution.py:25
  110.1 0.0 copy-done.1
  110.1 0.0 copy-done.2
  110.1 5.0 %fusion.2 = bf16[128,4096]{1,0:T(8,128)(2,1)} fusion(bf16[4096,512]{1,0:T(8,128)(2,1)} %param.9, bf16[1024,4096]{1,0:T(8,128)(2,1)} %param.8, s32[]{:T(128)S(6)} %select_n.4, f32[128,512]{1,0:T(8,128)} %reduce-scatter.3.cloned.1.call-done, f32[1,128,512]{2,1,0:T(8,128)S(1)} %copy-done.1, f32[1,128,512]{2,1,0:T(8,128)S(1)} %copy-done.2), kind=kOutput, calls=%fused_computation.4 | convolution fusion | flops 539688960 | bytes 7077892 | tf_op jit(solution)/shard_map/dot_general | solution.py:41
  115.1 0.0 all-gather.6.cloned.1.call-update
  115.1 0.0 reduce-scatter.5.cloned.1.call-start
  115.2 2.9 fusion.12
  118.1 51.5 %all-gather.6.cloned.1.call-done = bf16[1024,4096]{1,0:T(8,128)(2,1)} async-done(((bf16[128,4096]{1,0:T(8,128)(2,1)}), bf16[1024,4096]{1,0:T(8,128)(2,1)}) %all-gather.6.cloned.1.call-update) | async-done | bytes 8388624 | tf_op jit(solution)/shard_map/all_gather | solution.py:45
  169.5 6.3 %fusion.7 = bf16[128,1024]{1,0:T(8,128)(2,1)S(1)} fusion(bf16[1024,4096]{1,0:T(8,128)(2,1)} %all-gather.6.cloned.1.call-done, bf16[2,128,4096]{2,1,0:T(8,128)(2,1)S(1)} %copy-done, bf16[2,128,1024]{2,1,0:T(8,128)(2,1)S(1)} %copy-done.5), kind=kOutput, calls=%fused_computation.10 | convolution fusion | flops 1074397184 | bytes 9961472 | tf_op jit(solution)/shard_map/dot_general | solution.py:16
  175.8 0.0 copy-start.3
  175.8 2.4 fusion.25
  178.2 0.0 reduce-scatter.5.cloned.1.call-update
  178.2 0.0 all-gather.8.cloned.1.call-start
  178.2 41.2 %reduce-scatter.5.cloned.1.call-done = f32[128,512]{1,0:T(8,128)} async-done(((f32[1024,512]{1,0:T(8,128)}), f32[128,512]{1,0:T(8,128)}) %reduce-scatter.5.cloned.1.call-update) | async-done | bytes 262160 | tf_op jit(solution)/shard_map/reduce_scatter | solution.py:25
  219.4 0.0 copy-done.3
  219.4 0.0 copy-start.4
  219.4 5.1 %fusion.3 = bf16[128,4096]{1,0:T(8,128)(2,1)} fusion(bf16[4096,512]{1,0:T(8,128)(2,1)} %param.9, bf16[1024,4096]{1,0:T(8,128)(2,1)} %all-gather.6.cloned.1.call-done, s32[]{:T(128)S(6)} %select_n.4, f32[128,512]{1,0:T(8,128)} %reduce-scatter.5.cloned.1.call-done, f32[128,512]{1,0:T(8,128)S(1)} %copy-done.3, f32[1,128,512]{2,1,0:T(8,128)S(1)} %copy-done.1, ...), kind=kOutput, calls=%fused_computation.5 | convolution fusion | flops 540213248 | bytes 7340036 | tf_op jit(solution)/shard_map/dot_general | solution.py:41
  224.5 0.0 all-gather.8.cloned.1.call-update
  224.6 0.0 copy-done.4
  224.6 0.9 fusion.16
  225.5 53.5 %all-gather.8.cloned.1.call-done = bf16[1024,4096]{1,0:T(8,128)(2,1)} async-done(((bf16[128,4096]{1,0:T(8,128)(2,1)}), bf16[1024,4096]{1,0:T(8,128)(2,1)}) %all-gather.8.cloned.1.call-update) | async-done | bytes 8388624 | tf_op jit(solution)/shard_map/all_gather | solution.py:45
  279.0 7.9 %copy.10 = bf16[1024,4096]{1,0:T(8,128)(2,1)} copy(bf16[1024,4096]{1,0:T(8,128)(2,1)} %all-gather.8.cloned.1.call-done) | data formatting | bytes 16777216
Async XLA Ops:
  7.2 54.2 %copy-start.5 = (bf16[2,128,1024]{2,1,0:T(8,128)(2,1)S(1)}, bf16[2,128,1024]{2,1,0:T(8,128)(2,1)}, u32[]{:S(2)}) copy-start(bf16[2,128,1024]{2,1,0:T(8,128)(2,1)} %param.7) | copy-start | bytes 1572868
  7.2 50.8 %all-gather.4.cloned.1.call-start = ((), (), s32[]{:S(2)}) async-start(), calls=%async_computation.2 | async-start | bytes 2621440 | tf_op jit(solution)/shard_map/all_gather | solution.py:8
  7.9 102.2 %reduce-scatter.3.cloned.1.call-start = ((), (), s32[]{:S(2)}) async-start(), calls=%async_computation.3 | async-start | bytes 2359296 | tf_op jit(solution)/shard_map/reduce_scatter | solution.py:25
  58.0 3.4 %copy-start = (bf16[2,128,4096]{2,1,0:T(8,128)(2,1)S(1)}, bf16[2,128,4096]{2,1,0:T(8,128)(2,1)}, u32[]{:S(2)}) copy-start(bf16[2,128,4096]{2,1,0:T(8,128)(2,1)} %all-gather.4.cloned.1.call-done) | copy-start | bytes 6291460
  67.6 42.5 %copy-start.1 = (f32[1,128,512]{2,1,0:T(8,128)S(1)}, f32[1,128,512]{2,1,0:T(8,128)}, u32[]{:S(2)}) copy-start(f32[1,128,512]{2,1,0:T(8,128)} %param.10) | copy-start | bytes 786436
  67.6 42.5 %copy-start.2 = (f32[1,128,512]{2,1,0:T(8,128)S(1)}, f32[1,128,512]{2,1,0:T(8,128)}, u32[]{:S(2)}) copy-start(f32[1,128,512]{2,1,0:T(8,128)} %param.11) | copy-start | bytes 786436
  70.0 99.5 %all-gather.6.cloned.1.call-start = ((), (), s32[]{:S(2)}) async-start(), calls=%async_computation.4 | async-start | bytes 9437184 | tf_op jit(solution)/shard_map/all_gather | solution.py:45
  115.1 104.3 %reduce-scatter.5.cloned.1.call-start = ((), (), s32[]{:S(2)}) async-start(), calls=%async_computation.5 | async-start | bytes 2359296 | tf_op jit(solution)/shard_map/reduce_scatter | solution.py:25
  175.8 43.6 %copy-start.3 = (f32[128,512]{1,0:T(8,128)S(1)}, f32[128,512]{1,0:T(8,128)}, u32[]{:S(2)}) copy-start(f32[128,512]{1,0:T(8,128)} %reduce-scatter.3.cloned.1.call-done) | copy-start | bytes 786436
  178.2 100.8 %all-gather.8.cloned.1.call-start = ((), (), s32[]{:S(2)}) async-start(), calls=%async_computation.6 | async-start | bytes 9437184 | tf_op jit(solution)/shard_map/all_gather | solution.py:45
  219.4 5.1 %copy-start.4 = (f32[128,512]{1,0:T(8,128)S(1)}, f32[128,512]{1,0:T(8,128)}, u32[]{:S(2)}) copy-start(f32[128,512]{1,0:T(8,128)} %reduce-scatter.5.cloned.1.call-done) | copy-start | bytes 786436
Sparse Core Ops, SparseCore 0:
  9.6 48.3 all-gather.3
  70.2 39.9 reduce-scatter.2
  115.2 54.2 all-gather.5
  178.3 41.0 reduce-scatter.4
  224.7 54.2 all-gather.7
where the time goes:
time: 294 us; the launch traced here: 293 us
  waiting for transfers between devices  237 us (81%)
  matrix products  33.6 us (11%)
  between operations  13.9 us (5%)
  local copies, waits for them, and re-layouts  7.91 us (3%)
    all_gather x2, waiting for transfers between devices, local(): current = lax.all_gather(new_rows, 'dp', axis=0, tiled=True)  105 us
    reduce_scatter x2, waiting for transfers between devices, local(): lax.psum_scatter(lax.dot_general(part_errors, reduced, (((0,), (0,)), (()...  81.2 us
    all_gather x1, waiting for transfers between devices, local(): whole = lax.all_gather(tokens, 'mp', axis=2, tiled=True)  50 us
    dot_general x2, matrix products, local(): lax.dot_general(inputs, current, (((1,), (1,)), ((), ())), preferred_elem...  12.5 us
    dot_general x2, matrix products, local(): lax.dot_general(direction, basis, (((1,), (1,)), ((), ())), preferred_ele...  10.1 us
    unnamed x13, local copies, waits for them, and re-layouts  7.91 us
    dot_general x2, matrix products, local(): reduced = jnp.dot(inputs, basis, preferred_element_type=jnp.float32)  6.28 us
  transfers between devices with their start and end apart: 5, of which 5 were waited for; matrix products, arithmetic and copies ran while one was open for 1% of the time, Pallas kernels for 0%

commit v1 on v0

--- a/solution.py
+++ b/solution.py
@@ -5,7 +5,12 @@
 
 
 def local(tokens, targets, weight, basis, moment1, moment2):
-    whole = lax.all_gather(tokens, "mp", axis=2, tiled=True)
+    ring = [tokens]
+    for hop in range(3):
+        ring.append(lax.ppermute(ring[-1], "mp", [(dev, (dev + 1) % 4) for dev in range(4)]))
+    whole = jnp.roll(
+        jnp.concatenate(ring[::-1], axis=2), (lax.axis_index("mp") + 1) * ring[0].shape[2], axis=2
+    )
     total_tokens = tokens.shape[1] * lax.axis_size("dp")
     owned_rows = moment1.shape[1]
     first = moment1[0]

time: 294 us -> 288 us (0.980)
  waiting for transfers between devices: 237 us -> 228 us
  local copies, waits for them, and re-layouts: 7.91 us -> 13.4 us
  matrix products: 33.6 us -> 28.4 us
  starting transfers between devices: 0.2 us -> 3.27 us
    all_gather x1 -> x0, waiting for transfers between devices: 50 us -> none  [local(): whole = lax.all_gather(tokens, 'mp', axis=2, tiled=True)]
    ppermute x0 -> x3, waiting for transfers between devices: none -> 43.1 us  [local(): lax.ppermute(ring[-1], 'mp', [(dev, (dev + 1) % 4) for dev in range(4)])]
    unnamed x13 -> x26, local copies, waits for them, and re-layouts: 7.91 us -> 13.4 us
    ppermute x0 -> x3, starting transfers between devices: none -> 3.11 us  [local(): lax.ppermute(ring[-1], 'mp', [(dev, (dev + 1) % 4) for dev in range(4)])]
    dot_general x2, matrix products: 12.5 us -> 9.51 us  [local(): lax.dot_general(inputs, current, (((1,), (1,)), ((), ())), preferred_elem...]
  transfers between devices with their start and end apart: 5 -> 7, of which waited for: 5 -> 7; matrix products, arithmetic and copies ran while one was open for 1% -> 1% of each run, Pallas kernels for 0% -> 0%
where the time goes in v1:
time: 288 us
  waiting for transfers between devices  228 us (79%)
  matrix products  28.4 us (10%)
  between operations  13.9 us (5%)
  local copies, waits for them, and re-layouts  13.4 us (5%)
  starting transfers between devices  3.27 us (1%)
    all_gather x2, waiting for transfers between devices, local(): current = lax.all_gather(new_rows, 'dp', axis=0, tiled=True)  105 us
    reduce_scatter x2, waiting for transfers between devices, local(): lax.psum_scatter(lax.dot_general(part_errors, reduced, (((0,), (0,)), (()...  80.2 us
    ppermute x3, waiting for transfers between devices, local(): lax.ppermute(ring[-1], 'mp', [(dev, (dev + 1) % 4) for dev in range(4)])  43.1 us
    unnamed x26, local copies, waits for them, and re-layouts  13.4 us
    dot_general x2, matrix products, local(): lax.dot_general(direction, basis, (((1,), (1,)), ((), ())), preferred_ele...  10.2 us
    dot_general x2, matrix products, local(): lax.dot_general(inputs, current, (((1,), (1,)), ((), ())), preferred_elem...  9.51 us
  transfers between devices with their start and end apart: 7, of which 7 were waited for; matrix products, arithmetic and copies ran while one was open for 1% of the time, Pallas kernels for 0%

profile of v1, /device:TPU:0, one launch (start us, length us, event | category | flops | bytes accessed | tf_op | source)
XLA Modules:
  0.0 287.8 jit_solution(2537104762573849603)
XLA Ops:
  7.2 0.0 copy-start.6
  7.2 0.0 reduce-scatter.3.cloned.1.call-start
  7.2 3.1 %collective-permute-start = (bf16[2,128,1024]{2,1,0:T(8,128)(2,1)}, bf16[2,128,1024]{2,1,0:T(8,128)(2,1)S(1)}, u32[]{:S(2)}, u32[]{:S(2)}) collective-permute-start(bf16[2,128,1024]{2,1,0:T(8,128)(2,1)} %param.6), channel_id=1, source_target_pairs={{0,1},{1,2},{2,3},{3,0},{4,5},{5,6},{6,7},{7,4},{8,9},{9,10},{10,1... | collective-permute-start | bytes 1572872 | tf_op jit(solution)/shard_map/ppermute | solution.py:10
  10.3 14.2 %collective-permute-done = bf16[2,128,1024]{2,1,0:T(8,128)(2,1)S(1)} collective-permute-done((bf16[2,128,1024]{2,1,0:T(8,128)(2,1)}, bf16[2,128,1024]{2,1,0:T(8,128)(2,1)S(1)}, u32[]{:S(2)}, u32[]{:S(2)}) %collective-permute-start) | collective-permute-done | bytes 524320 | tf_op jit(solution)/shard_map/ppermute | solution.py:10
  24.5 0.0 collective-permute-start.1
  24.5 14.9 %collective-permute-done.1 = bf16[2,128,1024]{2,1,0:T(8,128)(2,1)S(1)} collective-permute-done((bf16[2,128,1024]{2,1,0:T(8,128)(2,1)S(1)}, bf16[2,128,1024]{2,1,0:T(8,128)(2,1)S(1)}, u32[]{:S(2)}, u32[]{:S(2)}) %collective-permute-start.1) | collective-permute-done | bytes 524320 | tf_op jit(solution)/shard_map/ppermute | solution.py:10
  39.4 0.0 collective-permute-start.2
  39.4 0.0 copy-start
  39.4 14.0 %collective-permute-done.2 = bf16[2,128,1024]{2,1,0:T(8,128)(2,1)S(1)} collective-permute-done((bf16[2,128,1024]{2,1,0:T(8,128)(2,1)S(1)}, bf16[2,128,1024]{2,1,0:T(8,128)(2,1)S(1)}, u32[]{:S(2)}, u32[]{:S(2)}) %collective-permute-start.2) | collective-permute-done | bytes 524320 | tf_op jit(solution)/shard_map/ppermute | solution.py:10
  53.5 1.1 constant_dynamic-update-slice_fusion.4
  54.6 0.0 copy-start.8
  54.7 0.0 copy-start.1
  54.8 0.0 copy-done.6
  54.8 0.0 copy-done
  54.8 0.0 copy-start.2
  54.9 0.7 fusion.10
  55.6 0.1 copy-done.8
  55.7 4.0 %copy-done.1 = bf16[1024,4096]{1,0:T(8,128)(2,1)S(1)} copy-done((bf16[1024,4096]{1,0:T(8,128)(2,1)S(1)}, bf16[1024,4096]{1,0:T(8,128)(2,1)}, u32[]{:S(2)}) %copy-start.1) | copy-done | bytes 8388632
  59.7 2.9 %fusion.9 = bf16[128,1024]{1,0:T(8,128)(2,1)S(1)} fusion(bf16[1024,4096]{1,0:T(8,128)(2,1)S(1)} %copy-done.1, bf16[2,128,8192]{2,1,0:T(8,128)(2,1)S(1)} %constant_dynamic-update-slice_fusion, s32[]{:T(128)S(6)} %select_n.19, bf16[2,128,1024]{2,1,0:T(8,128)(2,1)S(1)} %copy-done.8), kind=kOutput, calls=%fused_computation.13 | convolution fusion | flops 1074397184 | bytes 9961476 | tf_op jit(solution)/shard_map/dot_general | solution.py:21
  62.6 0.0 copy-done.2
  62.6 0.0 copy-start.3
  62.6 0.0 copy-start.4
  62.6 2.4 fusion.27
  65.0 0.0 reduce-scatter.3.cloned.1.call-update
  65.0 0.0 all-gather.3.cloned.1.call-start
  65.1 39.0 %reduce-scatter.3.cloned.1.call-done = f32[128,512]{1,0:T(8,128)} async-done(((f32[1024,512]{1,0:T(8,128)}), f32[128,512]{1,0:T(8,128)}) %reduce-scatter.3.cloned.1.call-update) | async-done | bytes 262160 | tf_op jit(solution)/shard_map/reduce_scatter | solution.py:30
  104.1 0.0 copy-done.3
  104.1 0.0 copy-done.4
  104.1 5.1 %fusion.2 = bf16[128,4096]{1,0:T(8,128)(2,1)} fusion(bf16[4096,512]{1,0:T(8,128)(2,1)} %param.9, bf16[1024,4096]{1,0:T(8,128)(2,1)} %param.8, s32[]{:T(128)S(6)} %select_n.17, f32[128,512]{1,0:T(8,128)} %reduce-scatter.3.cloned.1.call-done, f32[1,128,512]{2,1,0:T(8,128)S(1)} %copy-done.3, f32[1,128,512]{2,1,0:T(8,128)S(1)} %copy-done.4), kind=kOutput, calls=%fused_computation.4 | convolution fusion | flops 539688960 | bytes 7077892 | tf_op jit(solution)/shard_map/dot_general | solution.py:46
  109.2 0.0 all-gather.3.cloned.1.call-update
  109.2 0.0 reduce-scatter.5.cloned.1.call-start
  109.3 3.2 %fusion.11 = f32[128,512]{1,0:T(8,128)S(1)} fusion(bf16[4096,512]{1,0:T(8,128)(2,1)} %param.9, bf16[2,128,8192]{2,1,0:T(8,128)(2,1)} %copy-done.2, s32[]{:T(128)S(6)} %add.49, s32[]{:T(128)S(6)} %select_n.19), kind=kOutput, calls=%fused_computation.17 | convolution fusion | flops 536870912 | bytes 5505032 | tf_op jit(solution)/shard_map/dot_general | solution.py:27
  112.5 51.1 %all-gather.3.cloned.1.call-done = bf16[1024,4096]{1,0:T(8,128)(2,1)} async-done(((bf16[128,4096]{1,0:T(8,128)(2,1)}), bf16[1024,4096]{1,0:T(8,128)(2,1)}) %all-gather.3.cloned.1.call-update) | async-done | bytes 8388624 | tf_op jit(solution)/shard_map/all_gather | solution.py:50
  163.6 6.6 %fusion.6 = bf16[128,1024]{1,0:T(8,128)(2,1)S(1)} fusion(bf16[1024,4096]{1,0:T(8,128)(2,1)} %all-gather.3.cloned.1.call-done, bf16[2,128,8192]{2,1,0:T(8,128)(2,1)} %copy-done.2, s32[]{:T(128)S(6)} %add.49, s32[]{:T(128)S(6)} %select_n.19, bf16[2,128,1024]{2,1,0:T(8,128)(2,1)S(1)} %copy-done.8), kind=kOutput, calls=%fused_computation.9 | convolution fusion | flops 1074397184 | bytes 9961480 | tf_op jit(solution)/shard_map/dot_general | solution.py:21
  170.2 0.0 copy-start.5
  170.2 2.4 fusion.28
  172.6 0.0 reduce-scatter.5.cloned.1.call-update
  172.6 0.0 all-gather.5.cloned.1.call-start
  172.7 41.2 %reduce-scatter.5.cloned.1.call-done = f32[128,512]{1,0:T(8,128)} async-done(((f32[1024,512]{1,0:T(8,128)}), f32[128,512]{1,0:T(8,128)}) %reduce-scatter.5.cloned.1.call-update) | async-done | bytes 262160 | tf_op jit(solution)/shard_map/reduce_scatter | solution.py:30
  213.9 0.0 copy-done.5
  213.9 0.0 copy-start.7
  213.9 5.1 %fusion.3 = bf16[128,4096]{1,0:T(8,128)(2,1)} fusion(bf16[4096,512]{1,0:T(8,128)(2,1)} %param.9, bf16[1024,4096]{1,0:T(8,128)(2,1)} %all-gather.3.cloned.1.call-done, s32[]{:T(128)S(6)} %select_n.17, f32[128,512]{1,0:T(8,128)} %reduce-scatter.5.cloned.1.call-done, f32[128,512]{1,0:T(8,128)S(1)} %copy-done.5, f32[1,128,512]{2,1,0:T(8,128)S(1)} %copy-done.3, ...), kind=kOutput, calls=%fused_computation.5 | convolution fusion | flops 540213248 | bytes 7340036 | tf_op jit(solution)/shard_map/dot_general | solution.py:46
  219.0 0.0 all-gather.5.cloned.1.call-update
  219.0 0.0 copy-done.7
  219.0 0.9 fusion.15
  220.0 53.4 %all-gather.5.cloned.1.call-done = bf16[1024,4096]{1,0:T(8,128)(2,1)} async-done(((bf16[128,4096]{1,0:T(8,128)(2,1)}), bf16[1024,4096]{1,0:T(8,128)(2,1)}) %all-gather.5.cloned.1.call-update) | async-done | bytes 8388624 | tf_op jit(solution)/shard_map/all_gather | solution.py:50
  273.4 7.9 %copy.17 = bf16[1024,4096]{1,0:T(8,128)(2,1)} copy(bf16[1024,4096]{1,0:T(8,128)(2,1)} %all-gather.5.cloned.1.call-done) | data formatting | bytes 16777216
  (7 shorter events, 0.3 us)
Async XLA Ops:
  7.2 47.6 %copy-start.6 = (bf16[2,128,1024]{2,1,0:T(8,128)(2,1)S(1)}, bf16[2,128,1024]{2,1,0:T(8,128)(2,1)}, u32[]{:S(2)}) copy-start(bf16[2,128,1024]{2,1,0:T(8,128)(2,1)} %param.6) | copy-start | bytes 1572868
  7.2 96.9 %reduce-scatter.3.cloned.1.call-start = ((), (), s32[]{:S(2)}) async-start(), calls=%async_computation.2 | async-start | bytes 2359296 | tf_op jit(solution)/shard_map/reduce_scatter | solution.py:30
  7.2 17.3 %collective-permute-start = (bf16[2,128,1024]{2,1,0:T(8,128)(2,1)}, bf16[2,128,1024]{2,1,0:T(8,128)(2,1)S(1)}, u32[]{:S(2)}, u32[]{:S(2)}) collective-permute-start(bf16[2,128,1024]{2,1,0:T(8,128)(2,1)} %param.6), channel_id=1, source_target_pairs={{0,1},{1,2},{2,3},{3,0},{4,5},{5,6},{6,7},{7,4},{8,9},{9,10},{10,1... | collective-permute-start | bytes 1572872 | tf_op jit(solution)/shard_map/ppermute | solution.py:10
  24.5 14.9 %collective-permute-start.1 = (bf16[2,128,1024]{2,1,0:T(8,128)(2,1)S(1)}, bf16[2,128,1024]{2,1,0:T(8,128)(2,1)S(1)}, u32[]{:S(2)}, u32[]{:S(2)}) collective-permute-start(bf16[2,128,1024]{2,1,0:T(8,128)(2,1)S(1)} %collective-permute-done), channel_id=1, source_target_pairs={{0,1},{1,2},{2,3},{3,0},{4,5},{5,6},{6,7},{7,4},{8,9},{9,10},{10,1... | collective-permute-start | bytes 1572872 | tf_op jit(solution)/shard_map/ppermute | solution.py:10
  39.4 14.0 %collective-permute-start.2 = (bf16[2,128,1024]{2,1,0:T(8,128)(2,1)S(1)}, bf16[2,128,1024]{2,1,0:T(8,128)(2,1)S(1)}, u32[]{:S(2)}, u32[]{:S(2)}) collective-permute-start(bf16[2,128,1024]{2,1,0:T(8,128)(2,1)S(1)} %collective-permute-done.1), channel_id=1, source_target_pairs={{0,1},{1,2},{2,3},{3,0},{4,5},{5,6},{6,7},{7,4},{8,9},{9,10},{10,1... | collective-permute-start | bytes 1572872 | tf_op jit(solution)/shard_map/ppermute | solution.py:10
  39.4 15.5 %copy-start = (bf16[4096,512]{1,0:T(8,128)(2,1)S(1)}, bf16[4096,512]{1,0:T(8,128)(2,1)}, u32[]{:S(2)}) copy-start(bf16[4096,512]{1,0:T(8,128)(2,1)} %param.9) | copy-start | bytes 12582916
  54.6 1.0 copy-start.8
  54.7 5.0 %copy-start.1 = (bf16[1024,4096]{1,0:T(8,128)(2,1)S(1)}, bf16[1024,4096]{1,0:T(8,128)(2,1)}, u32[]{:S(2)}) copy-start(bf16[1024,4096]{1,0:T(8,128)(2,1)} %param.8) | copy-start | bytes 25165828
  54.8 7.8 %copy-start.2 = (bf16[2,128,8192]{2,1,0:T(8,128)(2,1)}, bf16[2,128,8192]{2,1,0:T(8,128)(2,1)S(1)}, u32[]{:S(2)}) copy-start(bf16[2,128,8192]{2,1,0:T(8,128)(2,1)S(1)} %constant_dynamic-update-slice_fusion) | copy-start | bytes 12582916
  62.6 41.5 %copy-start.3 = (f32[1,128,512]{2,1,0:T(8,128)S(1)}, f32[1,128,512]{2,1,0:T(8,128)}, u32[]{:S(2)}) copy-start(f32[1,128,512]{2,1,0:T(8,128)} %param.10) | copy-start | bytes 786436
  62.6 41.5 %copy-start.4 = (f32[1,128,512]{2,1,0:T(8,128)S(1)}, f32[1,128,512]{2,1,0:T(8,128)}, u32[]{:S(2)}) copy-start(f32[1,128,512]{2,1,0:T(8,128)} %param.11) | copy-start | bytes 786436
  65.0 98.6 %all-gather.3.cloned.1.call-start = ((), (), s32[]{:S(2)}) async-start(), calls=%async_computation.3 | async-start | bytes 9437184 | tf_op jit(solution)/shard_map/all_gather | solution.py:50
  109.2 104.7 %reduce-scatter.5.cloned.1.call-start = ((), (), s32[]{:S(2)}) async-start(), calls=%async_computation.4 | async-start | bytes 2359296 | tf_op jit(solution)/shard_map/reduce_scatter | solution.py:30
  170.2 43.6 %copy-start.5 = (f32[128,512]{1,0:T(8,128)S(1)}, f32[128,512]{1,0:T(8,128)}, u32[]{:S(2)}) copy-start(f32[128,512]{1,0:T(8,128)} %reduce-scatter.3.cloned.1.call-done) | copy-start | bytes 786436
  172.6 100.8 %all-gather.5.cloned.1.call-start = ((), (), s32[]{:S(2)}) async-start(), calls=%async_computation.5 | async-start | bytes 9437184 | tf_op jit(solution)/shard_map/all_gather | solution.py:50
  213.9 5.1 %copy-start.7 = (f32[128,512]{1,0:T(8,128)S(1)}, f32[128,512]{1,0:T(8,128)}, u32[]{:S(2)}) copy-start(f32[128,512]{1,0:T(8,128)} %reduce-scatter.5.cloned.1.call-done) | copy-start | bytes 786436
Sparse Core Ops, SparseCore 0:
  65.2 38.9 reduce-scatter.2
  109.3 54.2 all-gather.2
  172.7 41.0 reduce-scatter.4
  219.1 54.2 all-gather.4
